TPU v7x, 128 devices: a whole 4x4x4 slice. The times are simulated.
128 devices in a mesh: req: 32 (over z, x, core), tp: 4 (over y).
Axes of the slice: x: 4, y: 4, z: 4, core: 2. Of those that a mesh axis runs over, the one named last changes fastest.
Arguments:
- tokens: bfloat16 [12288, 5120], P('req'), may hold values from -40 to 40
- w_query: bfloat16 [5120, 2560], P(None, 'tp'), may hold values from -0.125 to 0.125
- query_bias: float32 [2560], P('tp'), may hold values from -24 to 24
- w_keyval: bfloat16 [5120, 1024], P(None, 'tp'), may hold values from -0.21875 to 0.21875
- keyval_bias: float32 [1024], P('tp'), may hold values from -2.5 to 2.5
- w_out: bfloat16 [2560, 5120], P('tp'), may hold values from -0.25 to 0.25
- attn_gain: float32 [5120], replicated, may hold values from 0.25 to 1.75
- final_norm_gain: float32 [5120], replicated, may hold values from 0.25 to 1.75
- head_weight: bfloat16 [5120, 76032], P(None, ('req', 'tp')), may hold values from -0.25 to 0.25
- kv_pool: bfloat16 [851968, 4, 256], P('req', 'tp'), may hold values from -17 to 17
- cache_len: int32 [512], replicated, may hold values from 256 to 3072, as said below
Outputs:
- states: bfloat16 [12288, 5120], P('req', 'tp')
- new_kv: bfloat16 [12288, 4, 256], P('req', 'tp')
- row_norms: float32 [512], P('req')
- logit_max: float32 [512], replicated
- logits: float32 [512, 76032], P(None, ('req', 'tp'))
Inputs may be any that keep to these rules, and one draw needn't show every extreme that they name: `cache_len`: every cache holds 256 or 3072 rows. Exactly 64 requests hold 3072; requests i * 16 to i * 16 + 15 hold at most 8 of them for every i, and exactly 8 for some i, so their caches fill at most 26624 rows, and exactly 26624 for some i.
All inputs are finite; a program needn't handle non-finite values.
Results may differ from a plain program's by a relative error of at most 0.014.
Values may be sent and summed in bfloat16 or wider, within the bound.
A program may use at most 192 MiB of HBM per device.

v0:
```python
import math
import jax
import jax.numpy as jnp
from jax import lax
from jax.sharding import PartitionSpec as P

HD = 128
GROUP = 5
NEW = 24
LONG = 3072
THETA = 1000000.0
EPS = 1e-06
NEG = -1e30


def rope_rotate(vectors, positions):
    head_width = vectors.shape[-1]
    halfway = head_width // 2
    frequency = THETA ** (-(jnp.arange(halfway, dtype=jnp.float32) * (2.0 / head_width)))
    angles = positions[..., None] * frequency
    cosine = jnp.cos(angles)
    sine_part = jnp.sin(angles)
    front_part = vectors[..., :halfway]
    back_part = vectors[..., halfway:]
    return jnp.concatenate(
        [front_part * cosine - back_part * sine_part, back_part * cosine + front_part * sine_part],
        axis=-1,
    )


def online_update(state_in, scores, value_matrix):
    running_max, totals, weighted = state_in
    new_max = jnp.maximum(running_max, jnp.max(scores, axis=-1))
    rescale = jnp.exp(running_max - new_max)
    weight_matrix = jnp.exp(scores - new_max[..., None])
    totals = totals * rescale + jnp.sum(weight_matrix, axis=-1)
    weighted = weighted * rescale[..., None] + jnp.einsum(
        "amz,zav->amv",
        weight_matrix.astype(jnp.bfloat16),
        value_matrix,
        preferred_element_type=jnp.float32,
    )
    return (new_max, totals, weighted)


def attend_windows(query_rows, pool_part, leading_row, req_starts, req_lens, start_state):
    head_width = query_rows.shape[-1]
    kv_local = query_rows.shape[0]
    query_count = query_rows.shape[1]
    req_count = req_starts.shape[0]
    row_span = query_count // req_count
    part_rows = pool_part.shape[0]
    window_rows = min(LONG, part_rows)
    batch_size = math.gcd(req_count, 4)
    batch_count = req_count // batch_size

    def per_request(query_block, begin, length, state_max, state_totals, state_weighted):
        first = jnp.clip(begin - leading_row, 0, part_rows - window_rows)
        window = lax.dynamic_slice_in_dim(pool_part, first, window_rows, 0)
        row_index = leading_row + first + jnp.arange(window_rows, dtype=jnp.int32)
        inside = (row_index >= begin) & (row_index < begin + length)
        scores = jnp.einsum(
            "mjl,wml->mjw",
            query_block,
            window[..., :head_width],
            preferred_element_type=jnp.float32,
        )
        scores = jnp.where(inside[None, None, :], scores, -jnp.inf)
        return online_update(
            (state_max, state_totals, state_weighted), scores, window[..., head_width:]
        )

    def split_requests(array_in):
        moved = jnp.moveaxis(
            array_in.reshape((kv_local, req_count, row_span) + array_in.shape[2:]), 1, 0
        )
        return moved.reshape((batch_count, batch_size) + moved.shape[1:])

    def join_requests(array_in):
        merged = array_in.reshape((req_count,) + array_in.shape[2:])
        return jnp.moveaxis(merged, 0, 1).reshape((kv_local, query_count) + merged.shape[3:])

    def one_batch(inputs):
        return jax.vmap(per_request)(*inputs)

    batched = (
        split_requests(query_rows),
        req_starts.reshape(batch_count, batch_size),
        req_lens.reshape(batch_count, batch_size),
        split_requests(start_state[0]),
        split_requests(start_state[1]),
        split_requests(start_state[2]),
    )
    result = lax.map(one_batch, batched)
    return tuple((join_requests(part_state) for part_state in result))


def local(
    tokens,
    w_query,
    query_bias,
    w_keyval,
    keyval_bias,
    w_out,
    attn_gain,
    final_norm_gain,
    head_weight,
    kv_pool,
    cache_len,
):
    groups = lax.axis_size("req")
    my_group = lax.axis_index("req")
    tp_count = lax.axis_size("tp")
    tp_index = lax.axis_index("tp")
    tok_rows = tokens.shape[0]
    model_width = tokens.shape[1]
    per_group = tok_rows // NEW
    kv_local = kv_pool.shape[1]
    lens_grid = cache_len.reshape(groups, per_group)
    my_lens = lax.dynamic_slice_in_dim(lens_grid, my_group, 1, 0)[0]
    my_starts = jnp.cumsum(my_lens) - my_lens
    source = tokens.astype(jnp.float32)
    mean_square = jnp.mean(source * source, axis=1, keepdims=True)
    normed = (source / jnp.sqrt(mean_square + EPS) * attn_gain[None, :]).astype(jnp.bfloat16)
    query_raw = jnp.dot(normed, w_query, preferred_element_type=jnp.float32) + query_bias[None, :]
    keyval_raw = (
        jnp.dot(normed, w_keyval, preferred_element_type=jnp.float32) + keyval_bias[None, :]
    )
    positions = (my_lens[:, None] + jnp.arange(NEW, dtype=jnp.int32)[None, :]).astype(jnp.float32)
    query_heads = query_raw.reshape(per_group, NEW, kv_local, GROUP, HD)
    queries = (
        rope_rotate(query_heads, positions[:, :, None, None]) * (1.0 / math.sqrt(HD))
    ).astype(jnp.bfloat16)
    keyval_heads = keyval_raw.reshape(per_group, NEW, kv_local, 2, HD)
    key_new = rope_rotate(keyval_heads[:, :, :, 0, :], positions[:, :, None]).astype(jnp.bfloat16)
    value_new = keyval_heads[:, :, :, 1, :].astype(jnp.bfloat16)
    new_kv = jnp.concatenate([key_new, value_new], axis=-1).reshape(tok_rows, kv_local, 2 * HD)
    row_span = NEW * GROUP
    query_count = per_group * row_span
    query_rows = jnp.transpose(queries, (2, 0, 1, 3, 4)).reshape(kv_local, query_count, HD)
    start_state = (
        jnp.full((kv_local, query_count), NEG, jnp.float32),
        jnp.zeros((kv_local, query_count), jnp.float32),
        jnp.zeros((kv_local, query_count, HD), jnp.float32),
    )
    carry_state = attend_windows(query_rows, kv_pool, 0, my_starts, my_lens, start_state)
    key_rows = key_new.reshape(tok_rows, kv_local, HD)
    value_rows = value_new.reshape(tok_rows, kv_local, HD)
    new_scores = jnp.einsum(
        "kqd,mkd->kqm", query_rows, key_rows, preferred_element_type=jnp.float32
    )
    query_token = jnp.arange(query_count, dtype=jnp.int32) // GROUP
    key_token = jnp.arange(tok_rows, dtype=jnp.int32)
    allowed = (query_token[:, None] // NEW == key_token[None, :] // NEW) & (
        key_token[None, :] <= query_token[:, None]
    )
    new_scores = jnp.where(allowed[None], new_scores, -jnp.inf)
    carry_state = online_update(carry_state, new_scores, value_rows)
    attention = (carry_state[2] / carry_state[1][..., None]).astype(jnp.bfloat16)
    attention = jnp.transpose(
        attention.reshape(kv_local, per_group, NEW, GROUP, HD), (1, 2, 0, 3, 4)
    ).reshape(tok_rows, kv_local * GROUP * HD)
    partial_value = jnp.dot(attention, w_out, preferred_element_type=jnp.float32)
    width_local = model_width // tp_count
    summed = lax.psum(partial_value.astype(jnp.bfloat16), "tp").astype(jnp.float32)
    states_full = (source + summed).astype(jnp.bfloat16)
    states = lax.dynamic_slice_in_dim(states_full, tp_index * width_local, width_local, 1)
    last_rows = states_full.reshape(per_group, NEW, model_width)[:, NEW - 1, :].astype(jnp.float32)
    row_norms = jnp.sqrt(jnp.mean(last_rows * last_rows, axis=1) + EPS)
    final_rows = (last_rows / row_norms[:, None] * final_norm_gain[None, :]).astype(jnp.bfloat16)
    logits = jnp.dot(
        lax.all_gather(final_rows, "req", axis=0, tiled=True),
        head_weight,
        preferred_element_type=jnp.float32,
    )
    logit_max = lax.pmax(jnp.max(logits, axis=1), ("req", "tp"))
    return (states, new_kv, row_norms, logit_max, logits)


def solution(mesh):
    return jax.shard_map(
        local,
        mesh=mesh,
        in_specs=(
            P("req", None),
            P(None, "tp"),
            P("tp"),
            P(None, "tp"),
            P("tp"),
            P("tp", None),
            P(),
            P(),
            P(None, ("req", "tp")),
            P("req", "tp", None),
            P(),
        ),
        out_specs=(P("req", "tp"), P("req", "tp", None), P("req"), P(), P(None, ("req", "tp"))),
        check_vma=False,
    )
```

profile of v0, /device:TPU:1, one launch (start us, length us, event | category | flops | bytes accessed | tf_op | source)
XLA Modules:
  0.0 365.2 jit_solution(11805179985593253152)
XLA Ops:
  7.3 3.1 fusion.27
  10.7 3.6 fusion.29
  16.1 4.2 %convolution_add_fusion.1 = f32[384,640]{1,0:T(8,128)} fusion(bf16[384,5120]{1,0:T(8,128)(2,1)S(1)} %fusion.29, bf16[5120,640]{1,0:T(8,128)(2,1)S(1)} %copy-done.12, f32[640]{0:T(1024)S(1)} %copy-done.13), kind=kOutput, calls=%fused_computation.58 | convolution fusion | flops 2516828160 | bytes 11471360 | tf_op jit(solution)/shard_map/dot_general | solution.py:125
  23.5 4.2 %multiply_subtract_fusion = (f32[16,24,1,5,64]{4,3,1,0,2:T(8,128)}, f32[16,24,1,5,64]{4,3,1,0,2:T(8,128)}) fusion(f32[16,24,1,5,128]{4,3,1,0,2:T(8,128)} %reshape.555, f32[16,24,64]{2,1,0:T(8,128)S(1)} %get-tuple-element.120, f32[16,24,64]{2,1,0:T(8,128)S(1)} %get-tuple-element.119), kind=kLoop, calls=%fused_computation.56 | loop fusion | flops 737280 | bytes 2162688 | tf_op jit(solution)/shard_map/sub | solution.py:26
  38.9 3.3 convolution_add_fusion.2
  45.7 81.0 %while.17 = (s32[]{:T(128)}, f32[4,4,1,120]{3,1,2,0:T(4,128)S(1)}, f32[4,4,1,120]{3,1,2,0:T(4,128)S(1)}, f32[4,4,1,120,128]{4,3,1,2,0:T(8,128)}, s32[4,4]{1,0:T(...) while((s32[]{:T(128)}, f32[4,4,1,120]{3,1,2,0:T(4,128)S(1)}, ...), condition=%wide.region_5.6_spmd, body=%wide.region_2.5_spmd.sunk | while | flops 766884224 | bytes 52985684 | solution.py:94
  46.1 12.2 %while.18 = (s32[]{:T(128)}, bf16[26624,1,256]{2,0,1:T(8,128)(2,1)}, s32[4,3]{1,0:T(4,128)S(1)}, bf16[4,3072,1,256]{3,1,2,0:T(8,128)(2,1)}, s32[]{:T(128)}) while((s32[]{:T(128)}, bf16[26624,1,256]{2,0,1:T(8,128)(2,1)}, s32[4,3]{1,0:T(4,128)S(1)}, bf16[4,3072,1,256]{3,1,2,0:T(8,128)(2,1)}, s32[]{:T(128)}) %tuple.62), condition=%wide.while_cond, body=%wide.while_body.sunk | while | flops 2 | bytes 3145833 | solution.py:59
  46.1 3.2 bitcast_dynamic-update-slice_fusion.3
  55.3 3.0 bitcast_dynamic-update-slice_fusion.3
  58.3 4.2 %select_reduce_fusion.2 = (f32[4,120]{1,0:T(4,128)S(1)}, f32[4,120,3072]{2,1,0:T(8,128)S(1)}) fusion(pred[4,3072]{1,0:T(4,128)(4,1)S(1)} %fusion.90, bf16[4,3072,1,256]{3,1,0,2:T(8,128)(2,1)} %bitcast.118, bf16[1,4,1,120,128]{4,1,0,3,2:T(4,128)(2,1)S(1)} %constant_dynamic-slice_fusion.8), kind=kOutput, calls=%fused_computation.3.clone.1 | convolution fusion | flops 380436000 | bytes 9181056 | tf_op jit(solution)/shard_map/while/body/eval_jaxpr/vmap(mjl,wml->mjw)/dot_general | solution.py:62
  66.4 12.1 %while.18 = (s32[]{:T(128)}, bf16[26624,1,256]{2,0,1:T(8,128)(2,1)}, s32[4,3]{1,0:T(4,128)S(1)}, bf16[4,3072,1,256]{3,1,2,0:T(8,128)(2,1)}, s32[]{:T(128)}) while((s32[]{:T(128)}, bf16[26624,1,256]{2,0,1:T(8,128)(2,1)}, s32[4,3]{1,0:T(4,128)S(1)}, bf16[4,3072,1,256]{3,1,2,0:T(8,128)(2,1)}, s32[]{:T(128)}) %tuple.62), condition=%wide.while_cond, body=%wide.while_body.sunk | while | flops 2 | bytes 3145833 | solution.py:59
  75.4 3.0 bitcast_dynamic-update-slice_fusion.3
  78.4 4.2 %select_reduce_fusion.2 = (f32[4,120]{1,0:T(4,128)S(1)}, f32[4,120,3072]{2,1,0:T(8,128)S(1)}) fusion(pred[4,3072]{1,0:T(4,128)(4,1)S(1)} %fusion.90, bf16[4,3072,1,256]{3,1,0,2:T(8,128)(2,1)} %bitcast.118, bf16[1,4,1,120,128]{4,1,0,3,2:T(4,128)(2,1)S(1)} %constant_dynamic-slice_fusion.8), kind=kOutput, calls=%fused_computation.3.clone.1 | convolution fusion | flops 380436000 | bytes 9181056 | tf_op jit(solution)/shard_map/while/body/eval_jaxpr/vmap(mjl,wml->mjw)/dot_general | solution.py:62
  86.5 12.1 %while.18 = (s32[]{:T(128)}, bf16[26624,1,256]{2,0,1:T(8,128)(2,1)}, s32[4,3]{1,0:T(4,128)S(1)}, bf16[4,3072,1,256]{3,1,2,0:T(8,128)(2,1)}, s32[]{:T(128)}) while((s32[]{:T(128)}, bf16[26624,1,256]{2,0,1:T(8,128)(2,1)}, s32[4,3]{1,0:T(4,128)S(1)}, bf16[4,3072,1,256]{3,1,2,0:T(8,128)(2,1)}, s32[]{:T(128)}) %tuple.62), condition=%wide.while_cond, body=%wide.while_body.sunk | while | flops 2 | bytes 3145833 | solution.py:59
  95.6 3.0 bitcast_dynamic-update-slice_fusion.3
  98.6 4.2 %select_reduce_fusion.2 = (f32[4,120]{1,0:T(4,128)S(1)}, f32[4,120,3072]{2,1,0:T(8,128)S(1)}) fusion(pred[4,3072]{1,0:T(4,128)(4,1)S(1)} %fusion.90, bf16[4,3072,1,256]{3,1,0,2:T(8,128)(2,1)} %bitcast.118, bf16[1,4,1,120,128]{4,1,0,3,2:T(4,128)(2,1)S(1)} %constant_dynamic-slice_fusion.8), kind=kOutput, calls=%fused_computation.3.clone.1 | convolution fusion | flops 380436000 | bytes 9181056 | tf_op jit(solution)/shard_map/while/body/eval_jaxpr/vmap(mjl,wml->mjw)/dot_general | solution.py:62
  106.7 12.1 %while.18 = (s32[]{:T(128)}, bf16[26624,1,256]{2,0,1:T(8,128)(2,1)}, s32[4,3]{1,0:T(4,128)S(1)}, bf16[4,3072,1,256]{3,1,2,0:T(8,128)(2,1)}, s32[]{:T(128)}) while((s32[]{:T(128)}, bf16[26624,1,256]{2,0,1:T(8,128)(2,1)}, s32[4,3]{1,0:T(4,128)S(1)}, bf16[4,3072,1,256]{3,1,2,0:T(8,128)(2,1)}, s32[]{:T(128)}) %tuple.62), condition=%wide.while_cond, body=%wide.while_body.sunk | while | flops 2 | bytes 3145833 | solution.py:59
  118.7 4.2 %select_reduce_fusion.2 = (f32[4,120]{1,0:T(4,128)S(1)}, f32[4,120,3072]{2,1,0:T(8,128)S(1)}) fusion(pred[4,3072]{1,0:T(4,128)(4,1)S(1)} %fusion.90, bf16[4,3072,1,256]{3,1,0,2:T(8,128)(2,1)} %bitcast.118, bf16[1,4,1,120,128]{4,1,0,3,2:T(4,128)(2,1)S(1)} %constant_dynamic-slice_fusion.8), kind=kOutput, calls=%fused_computation.3.clone.1 | convolution fusion | flops 380436000 | bytes 9181056 | tf_op jit(solution)/shard_map/while/body/eval_jaxpr/vmap(mjl,wml->mjw)/dot_general | solution.py:62
  129.9 7.6 %convolution_convert_fusion = bf16[384,5120]{1,0:T(8,128)(2,1)} fusion(bf16[384,640]{1,0:T(8,128)(2,1)S(1)} %reshape_transpose_reshape.16, bf16[640,5120]{1,0:T(8,128)(2,1)} %param.18), kind=kOutput, calls=%fused_computation.45 | convolution fusion | flops 2518548480 | bytes 10977280 | tf_op jit(solution)/shard_map/dot_general | solution.py:163
  137.5 91.8 %all-reduce.3.cloned.1.call-done = bf16[384,5120]{1,0:T(8,128)(2,1)} async-done(((bf16[384,5120]{1,0:T(8,128)(2,1)}), bf16[384,5120]{1,0:T(8,128)(2,1)}) %all-reduce.3.cloned.1.call-update) | async-done | bytes 3932176 | tf_op jit(solution)/shard_map/psum | solution.py:165
  229.4 4.8 %fusion.30 = bf16[384,5120]{1,0:T(8,128)(2,1)S(1)} fusion(bf16[384,5120]{1,0:T(8,128)(2,1)} %param.13, bf16[384,5120]{1,0:T(8,128)(2,1)} %all-reduce.3.cloned.1.call-done), kind=kLoop, calls=%fused_computation.44 | loop fusion | flops 7864320 | bytes 11796480 | tf_op jit(solution)/shard_map/convert_element_type | solution.py:166
  240.4 44.9 %all-gather.2.cloned.1.call-done = bf16[512,5120]{1,0:T(8,128)(2,1)} async-done(((bf16[16,5120]{1,0:T(8,128)(2,1)}), bf16[512,5120]{1,0:T(8,128)(2,1)}) %all-gather.2.cloned.1.call-update) | async-done | bytes 5242896 | tf_op jit(solution)/shard_map/all_gather | solution.py:172
  285.3 8.8 %fusion.72 = (f32[512]{0:T(512)S(1)}, f32[512,594]{0,1:T(8,128)}) fusion(bf16[512,5120]{1,0:T(8,128)(2,1)} %all-gather.2.cloned.1.call-done, bf16[5120,594]{0,1:T(8,128)(2,1)} %param.21), kind=kOutput, calls=%fused_computation.122 | convolution fusion | flops 3114574336 | bytes 12544000 | tf_op jit(solution)/shard_map/dot_general | solution.py:171
  294.2 64.1 %pmax.7 = f32[512]{0:T(512)} all-reduce(f32[512]{0:T(512)S(1)} %get-tuple-element.123), channel_id=1, replica_groups=mesh['req'=32,'tp'=4] {'req','tp'}, use_global_device_ids=true, to_apply=%region_11.12 | all-reduce | flops 512 | bytes 4096 | tf_op jit(solution)/shard_map/pmax | solution.py:176
  (158 shorter events, 80.7 us)
Async XLA Ops:
  7.2 31.7 %copy-start = (bf16[5120,256]{1,0:T(8,128)(2,1)S(1)}, bf16[5120,256]{1,0:T(8,128)(2,1)}, u32[]{:S(2)}) copy-start(bf16[5120,256]{1,0:T(8,128)(2,1)} %param.16) | copy-start | bytes 7864324
  7.2 3.3 copy-start.10
  7.2 3.5 copy-start.8
  7.2 222.2 %all-reduce.3.cloned.1.call-start = ((), (), s32[]{:S(2)}) async-start(), calls=%async_computation | async-start | bytes 7864320 | tf_op jit(solution)/shard_map/psum | solution.py:165
  10.6 5.5 %copy-start.12 = (bf16[5120,640]{1,0:T(8,128)(2,1)S(1)}, bf16[5120,640]{1,0:T(8,128)(2,1)}, u32[]{:S(2)}) copy-start(bf16[5120,640]{1,0:T(8,128)(2,1)} %param.14) | copy-start | bytes 19660804
  10.7 5.5 %copy-start.13 = (f32[640]{0:T(1024)S(1)}, f32[640]{0:T(1024)}, u32[]{:S(2)}) copy-start(f32[640]{0:T(1024)} %param.15) | copy-start | bytes 7684
  14.2 1.9 copy-start.4
  30.1 8.8 %copy-start.14 = (f32[256]{0:T(256)S(1)}, f32[256]{0:T(256)}, u32[]{:S(2)}) copy-start(f32[256]{0:T(256)} %param.17) | copy-start | bytes 3076
  45.7 81.2 %copy-start.5 = (f32[1920,64]{1,0:T(8,128)S(1)}, f32[1920,64]{1,0:T(8,128)}, u32[]{:S(2)}) copy-start(f32[1920,64]{1,0:T(8,128)} %concatenate.59) | copy-start | bytes 1474564
  45.7 81.2 %copy-start.6 = (f32[1920,64]{1,0:T(8,128)S(1)}, f32[1920,64]{1,0:T(8,128)}, u32[]{:S(2)}) copy-start(f32[1920,64]{1,0:T(8,128)} %concatenate.60) | copy-start | bytes 1474564
  58.3 4.3 %copy-start.2 = (bf16[4,3072,1,256]{3,1,2,0:T(8,128)(2,1)S(1)}, bf16[4,3072,1,256]{3,1,2,0:T(8,128)(2,1)}, u32[]{:S(2)}) copy-start(bf16[4,3072,1,256]{3,1,2,0:T(8,128)(2,1)} %get-tuple-element.216) | copy-start | bytes 18874372 | tf_op jit(solution)/shard_map/while
  78.4 4.2 %copy-start.2 = (bf16[4,3072,1,256]{3,1,2,0:T(8,128)(2,1)S(1)}, bf16[4,3072,1,256]{3,1,2,0:T(8,128)(2,1)}, u32[]{:S(2)}) copy-start(bf16[4,3072,1,256]{3,1,2,0:T(8,128)(2,1)} %get-tuple-element.216) | copy-start | bytes 18874372 | tf_op jit(solution)/shard_map/while
  98.6 4.2 %copy-start.2 = (bf16[4,3072,1,256]{3,1,2,0:T(8,128)(2,1)S(1)}, bf16[4,3072,1,256]{3,1,2,0:T(8,128)(2,1)}, u32[]{:S(2)}) copy-start(bf16[4,3072,1,256]{3,1,2,0:T(8,128)(2,1)} %get-tuple-element.216) | copy-start | bytes 18874372 | tf_op jit(solution)/shard_map/while
  118.7 4.2 %copy-start.2 = (bf16[4,3072,1,256]{3,1,2,0:T(8,128)(2,1)S(1)}, bf16[4,3072,1,256]{3,1,2,0:T(8,128)(2,1)}, u32[]{:S(2)}) copy-start(bf16[4,3072,1,256]{3,1,2,0:T(8,128)(2,1)} %get-tuple-element.216) | copy-start | bytes 18874372 | tf_op jit(solution)/shard_map/while
  126.9 1.5 copy-start.7
  137.5 99.1 %copy-start.9 = (f32[5120]{0:T(1024)S(1)}, f32[5120]{0:T(1024)}, u32[]{:S(2)}) copy-start(f32[5120]{0:T(1024)} %param.20) | copy-start | bytes 61444
  137.5 147.8 %all-gather.2.cloned.1.call-start = ((), (), s32[]{:S(2)}) async-start(), calls=%async_computation.1 | async-start | bytes 5406720 | tf_op jit(solution)/shard_map/all_gather | solution.py:172
  234.2 1.9 copy-start.3
  236.6 57.6 %copy-start.11 = (f32[16]{0:T(128)}, f32[16]{0:T(128)S(1)}, u32[]{:S(2)}) copy-start(f32[16]{0:T(128)S(1)} %add_sqrt_fusion.1) | copy-start | bytes 196
  285.3 73.0 %copy-start.1 = (bf16[5120,256]{1,0:T(8,128)(2,1)S(1)}, bf16[5120,256]{1,0:T(8,128)(2,1)}, u32[]{:S(2)}) copy-start(bf16[5120,256]{1,0:T(8,128)(2,1)} %param.16) | copy-start | bytes 7864324
Sparse Core Ops, SparseCore 0:
  137.6 91.7 all-reduce.2
  237.5 47.7 all-gather.1
where the time goes:
time: 366 us; the launch traced here: 365 us
  waiting for transfers between devices  137 us (37%)
  local copies, waits for them, and re-layouts  69.7 us (19%)
  blocking collectives  64.1 us (18%)
  matrix products  51.4 us (14%)
  other arithmetic  28.1 us (8%)
  between operations  14.4 us (4%)
    psum x1, waiting for transfers between devices, local(): lax.psum(partial_value.astype(jnp.bfloat16), 'tp').astype(jnp.float32)  91.8 us
    pmax x1, blocking collectives, local(): logit_max = lax.pmax(jnp.max(logits, axis=1), ('req', 'tp'))  64.1 us
    gather x32, local copies, waits for them, and re-layouts  48.3 us
    all_gather x1, waiting for transfers between devices, local(): lax.all_gather(final_rows, 'req', axis=0, tiled=True)  44.9 us
    dot_general x4, matrix products, per_request(): jnp.einsum('mjl,wml->mjw', query_block, window[..., :head_width], preferr...  16.9 us
    dot_general x5, matrix products, online_update(): jnp.einsum('amz,zav->amv', weight_matrix.astype(jnp.bfloat16), value_matr...  9.56 us
    dot_general x1, matrix products, local(): jnp.dot(lax.all_gather(final_rows, 'req', axis=0, tiled=True), head_weigh...  8.84 us
    dot_general x1, matrix products, local(): jnp.dot(attention, w_out, preferred_element_type=jnp.float32)  7.58 us
  transfers between devices with their start and end apart: 2, of which 2 were waited for; matrix products, arithmetic and copies ran while one was open for 1% of the time, Pallas kernels for 0%

commit v1 on v0

--- a/solution.py
+++ b/solution.py
@@ -1,8 +1,10 @@
+import functools
 import math
 import jax
 import jax.numpy as jnp
 from jax import lax
 from jax.sharding import PartitionSpec as P
+from jax.lax import all_to_all, axis_size
 
 HD = 128
 GROUP = 5
@@ -11,6 +13,17 @@
 THETA = 1000000.0
 EPS = 1e-06
 NEG = -1e30
+
+
+def supply_cube_up(q_in, mesh_ax):
+    nd = axis_size(mesh_ax)
+    bank = tuple((nd if no == 0 else 1 for no in range(q_in.ndim)))
+    after = jnp.tile(q_in, bank)
+    v1 = all_to_all(after, mesh_ax, split_axis=0, concat_axis=0, tiled=True)
+    return v1
+
+
+_tell_lots_all = functools.partial(supply_cube_up, mesh_ax="req")
 
 
 def rope_rotate(vectors, positions):
@@ -168,11 +181,7 @@
     last_rows = states_full.reshape(per_group, NEW, model_width)[:, NEW - 1, :].astype(jnp.float32)
     row_norms = jnp.sqrt(jnp.mean(last_rows * last_rows, axis=1) + EPS)
     final_rows = (last_rows / row_norms[:, None] * final_norm_gain[None, :]).astype(jnp.bfloat16)
-    logits = jnp.dot(
-        lax.all_gather(final_rows, "req", axis=0, tiled=True),
-        head_weight,
-        preferred_element_type=jnp.float32,
-    )
+    logits = jnp.dot(_tell_lots_all(final_rows), head_weight, preferred_element_type=jnp.float32)
     logit_max = lax.pmax(jnp.max(logits, axis=1), ("req", "tp"))
     return (states, new_kv, row_norms, logit_max, logits)
 

time: 366 us -> 392 us (1.071)
  waiting for transfers between devices: 137 us -> 150 us
  starting transfers between devices: 0.08 us -> 7.76 us
    all_to_all x0 -> x1, waiting for transfers between devices: none -> 58.5 us  [supply_cube_up(): v1 = all_to_all(after, mesh_ax, split_axis=0, concat_axis=0, tiled=True)]
    all_gather x1 -> x0, waiting for transfers between devices: 44.9 us -> none  [local(): lax.all_gather(final_rows, 'req', axis=0, tiled=True)]
    all_to_all x0 -> x1, starting transfers between devices: none -> 7.72 us  [supply_cube_up(): v1 = all_to_all(after, mesh_ax, split_axis=0, concat_axis=0, tiled=True)]
where the time goes in v1:
time: 392 us; the launch traced here: 391 us
  waiting for transfers between devices  150 us (38%)
  local copies, waits for them, and re-layouts  72.6 us (19%)
  blocking collectives  66.5 us (17%)
  matrix products  51.4 us (13%)
  other arithmetic  27.4 us (7%)
  between operations  14.4 us (4%)
  starting transfers between devices  7.76 us (2%)
    psum x1, waiting for transfers between devices, local(): lax.psum(partial_value.astype(jnp.bfloat16), 'tp').astype(jnp.float32)  91.9 us
    pmax x1, blocking collectives, local(): logit_max = lax.pmax(jnp.max(logits, axis=1), ('req', 'tp'))  66.5 us
    all_to_all x1, waiting for transfers between devices, supply_cube_up(): v1 = all_to_all(after, mesh_ax, split_axis=0, concat_axis=0, tiled=True)  58.5 us
    gather x32, local copies, waits for them, and re-layouts  48.2 us
    dot_general x4, matrix products, per_request(): jnp.einsum('mjl,wml->mjw', query_block, window[..., :head_width], preferr...  16.9 us
    dot_general x5, matrix products, online_update(): jnp.einsum('amz,zav->amv', weight_matrix.astype(jnp.bfloat16), value_matr...  9.57 us
    dot_general x1, matrix products, local(): jnp.dot(_tell_lots_all(final_rows), head_weight, preferred_element_type=j...  8.84 us
  transfers between devices with their start and end apart: 2, of which 2 were waited for; matrix products, arithmetic and copies ran while one was open for 1% of the time, Pallas kernels for 0%

profile of v1, /device:TPU:1, one launch (start us, length us, event | category | flops | bytes accessed | tf_op | source)
XLA Modules:
  0.0 391.1 jit_solution(7699761293110443719)
XLA Ops:
  7.3 3.1 fusion.27
  10.7 3.6 fusion.29
  16.1 4.2 %convolution_add_fusion.1 = f32[384,640]{1,0:T(8,128)} fusion(bf16[384,5120]{1,0:T(8,128)(2,1)S(1)} %fusion.29, bf16[5120,640]{1,0:T(8,128)(2,1)S(1)} %copy-done.12, f32[640]{0:T(1024)S(1)} %copy-done.13), kind=kOutput, calls=%fused_computation.58 | convolution fusion | flops 2516828160 | bytes 11471360 | tf_op jit(solution)/shard_map/dot_general | solution.py:138
  23.5 4.1 %multiply_subtract_fusion = (f32[16,24,1,5,64]{4,3,1,0,2:T(8,128)}, f32[16,24,1,5,64]{4,3,1,0,2:T(8,128)}) fusion(f32[16,24,1,5,128]{4,3,1,0,2:T(8,128)} %reshape.593, f32[16,24,64]{2,1,0:T(8,128)S(1)} %get-tuple-element.120, f32[16,24,64]{2,1,0:T(8,128)S(1)} %get-tuple-element.119), kind=kLoop, calls=%fused_computation.56 | loop fusion | flops 737280 | bytes 2162688 | tf_op jit(solution)/shard_map/sub | solution.py:39
  38.9 3.3 convolution_add_fusion.2
  45.7 80.9 %while.17 = (s32[]{:T(128)}, f32[4,4,1,120]{3,1,2,0:T(4,128)S(1)}, f32[4,4,1,120]{3,1,2,0:T(4,128)S(1)}, f32[4,4,1,120,128]{4,3,1,2,0:T(8,128)}, s32[4,4]{1,0:T(...) while((s32[]{:T(128)}, f32[4,4,1,120]{3,1,2,0:T(4,128)S(1)}, ...), condition=%wide.region_5.6_spmd, body=%wide.region_2.5_spmd.sunk | while | flops 766884224 | bytes 52985684 | solution.py:107
  46.0 12.2 %while.18 = (s32[]{:T(128)}, bf16[26624,1,256]{2,0,1:T(8,128)(2,1)}, s32[4,3]{1,0:T(4,128)S(1)}, bf16[4,3072,1,256]{3,1,2,0:T(8,128)(2,1)}, s32[]{:T(128)}) while((s32[]{:T(128)}, bf16[26624,1,256]{2,0,1:T(8,128)(2,1)}, s32[4,3]{1,0:T(4,128)S(1)}, bf16[4,3072,1,256]{3,1,2,0:T(8,128)(2,1)}, s32[]{:T(128)}) %tuple.62), condition=%wide.while_cond, body=%wide.while_body.sunk | while | flops 2 | bytes 3145833 | solution.py:72
  46.1 3.2 bitcast_dynamic-update-slice_fusion.3
  55.2 3.0 bitcast_dynamic-update-slice_fusion.3
  58.3 4.2 %select_reduce_fusion.2 = (f32[4,120]{1,0:T(4,128)S(1)}, f32[4,120,3072]{2,1,0:T(8,128)S(1)}) fusion(pred[4,3072]{1,0:T(4,128)(4,1)S(1)} %fusion.90, bf16[4,3072,1,256]{3,1,0,2:T(8,128)(2,1)} %bitcast.119, bf16[1,4,1,120,128]{4,1,0,3,2:T(4,128)(2,1)S(1)} %constant_dynamic-slice_fusion.8), kind=kOutput, calls=%fused_computation.3.clone.1 | convolution fusion | flops 380436000 | bytes 9181056 | tf_op jit(solution)/shard_map/while/body/eval_jaxpr/vmap(mjl,wml->mjw)/dot_general | solution.py:75
  66.3 12.0 %while.18 = (s32[]{:T(128)}, bf16[26624,1,256]{2,0,1:T(8,128)(2,1)}, s32[4,3]{1,0:T(4,128)S(1)}, bf16[4,3072,1,256]{3,1,2,0:T(8,128)(2,1)}, s32[]{:T(128)}) while((s32[]{:T(128)}, bf16[26624,1,256]{2,0,1:T(8,128)(2,1)}, s32[4,3]{1,0:T(4,128)S(1)}, bf16[4,3072,1,256]{3,1,2,0:T(8,128)(2,1)}, s32[]{:T(128)}) %tuple.62), condition=%wide.while_cond, body=%wide.while_body.sunk | while | flops 2 | bytes 3145833 | solution.py:72
  75.4 3.0 bitcast_dynamic-update-slice_fusion.3
  78.4 4.2 %select_reduce_fusion.2 = (f32[4,120]{1,0:T(4,128)S(1)}, f32[4,120,3072]{2,1,0:T(8,128)S(1)}) fusion(pred[4,3072]{1,0:T(4,128)(4,1)S(1)} %fusion.90, bf16[4,3072,1,256]{3,1,0,2:T(8,128)(2,1)} %bitcast.119, bf16[1,4,1,120,128]{4,1,0,3,2:T(4,128)(2,1)S(1)} %constant_dynamic-slice_fusion.8), kind=kOutput, calls=%fused_computation.3.clone.1 | convolution fusion | flops 380436000 | bytes 9181056 | tf_op jit(solution)/shard_map/while/body/eval_jaxpr/vmap(mjl,wml->mjw)/dot_general | solution.py:75
  86.5 12.0 %while.18 = (s32[]{:T(128)}, bf16[26624,1,256]{2,0,1:T(8,128)(2,1)}, s32[4,3]{1,0:T(4,128)S(1)}, bf16[4,3072,1,256]{3,1,2,0:T(8,128)(2,1)}, s32[]{:T(128)}) while((s32[]{:T(128)}, bf16[26624,1,256]{2,0,1:T(8,128)(2,1)}, s32[4,3]{1,0:T(4,128)S(1)}, bf16[4,3072,1,256]{3,1,2,0:T(8,128)(2,1)}, s32[]{:T(128)}) %tuple.62), condition=%wide.while_cond, body=%wide.while_body.sunk | while | flops 2 | bytes 3145833 | solution.py:72
  98.5 4.2 %select_reduce_fusion.2 = (f32[4,120]{1,0:T(4,128)S(1)}, f32[4,120,3072]{2,1,0:T(8,128)S(1)}) fusion(pred[4,3072]{1,0:T(4,128)(4,1)S(1)} %fusion.90, bf16[4,3072,1,256]{3,1,0,2:T(8,128)(2,1)} %bitcast.119, bf16[1,4,1,120,128]{4,1,0,3,2:T(4,128)(2,1)S(1)} %constant_dynamic-slice_fusion.8), kind=kOutput, calls=%fused_computation.3.clone.1 | convolution fusion | flops 380436000 | bytes 9181056 | tf_op jit(solution)/shard_map/while/body/eval_jaxpr/vmap(mjl,wml->mjw)/dot_general | solution.py:75
  106.6 12.0 %while.18 = (s32[]{:T(128)}, bf16[26624,1,256]{2,0,1:T(8,128)(2,1)}, s32[4,3]{1,0:T(4,128)S(1)}, bf16[4,3072,1,256]{3,1,2,0:T(8,128)(2,1)}, s32[]{:T(128)}) while((s32[]{:T(128)}, bf16[26624,1,256]{2,0,1:T(8,128)(2,1)}, s32[4,3]{1,0:T(4,128)S(1)}, bf16[4,3072,1,256]{3,1,2,0:T(8,128)(2,1)}, s32[]{:T(128)}) %tuple.62), condition=%wide.while_cond, body=%wide.while_body.sunk | while | flops 2 | bytes 3145833 | solution.py:72
  118.6 4.2 %select_reduce_fusion.2 = (f32[4,120]{1,0:T(4,128)S(1)}, f32[4,120,3072]{2,1,0:T(8,128)S(1)}) fusion(pred[4,3072]{1,0:T(4,128)(4,1)S(1)} %fusion.90, bf16[4,3072,1,256]{3,1,0,2:T(8,128)(2,1)} %bitcast.119, bf16[1,4,1,120,128]{4,1,0,3,2:T(4,128)(2,1)S(1)} %constant_dynamic-slice_fusion.8), kind=kOutput, calls=%fused_computation.3.clone.1 | convolution fusion | flops 380436000 | bytes 9181056 | tf_op jit(solution)/shard_map/while/body/eval_jaxpr/vmap(mjl,wml->mjw)/dot_general | solution.py:75
  129.8 7.6 %convolution_convert_fusion = bf16[384,5120]{1,0:T(8,128)(2,1)} fusion(bf16[384,640]{1,0:T(8,128)(2,1)S(1)} %reshape_transpose_reshape.16, bf16[640,5120]{1,0:T(8,128)(2,1)} %param.18), kind=kOutput, calls=%fused_computation.45 | convolution fusion | flops 2518548480 | bytes 10977280 | tf_op jit(solution)/shard_map/dot_general | solution.py:176
  137.4 91.9 %all-reduce.3.cloned.1.call-done = bf16[384,5120]{1,0:T(8,128)(2,1)} async-done(((bf16[384,5120]{1,0:T(8,128)(2,1)}), bf16[384,5120]{1,0:T(8,128)(2,1)}) %all-reduce.3.cloned.1.call-update) | async-done | bytes 3932176 | tf_op jit(solution)/shard_map/psum | solution.py:178
  229.3 4.8 %fusion.30 = bf16[384,5120]{1,0:T(8,128)(2,1)S(1)} fusion(bf16[384,5120]{1,0:T(8,128)(2,1)} %param.13, bf16[384,5120]{1,0:T(8,128)(2,1)} %all-reduce.3.cloned.1.call-done), kind=kLoop, calls=%fused_computation.44 | loop fusion | flops 7864320 | bytes 11796480 | tf_op jit(solution)/shard_map/convert_element_type | solution.py:179
  239.6 7.7 %all-to-all-start = ((bf16[32,16,5120]{2,1,0:T(8,128)(2,1)}), bf16[32,16,5120]{2,1,0:T(8,128)(2,1)}, u32[]{:S(2)}, u32[]{:S(2)}) async-start(bf16[32,16,5120]{2,1,0:T(8,128)(2,1)} %tile.2), calls=%async_computation | async-start | bytes 10485760 | tf_op jit(solution)/shard_map/all_to_all | solution.py:22
  250.4 58.5 %all-to-all-done = bf16[32,16,5120]{2,1,0:T(8,128)(2,1)} async-done(((bf16[32,16,5120]{2,1,0:T(8,128)(2,1)}), bf16[32,16,5120]{2,1,0:T(8,128)(2,1)}, u32[]{:S(2)}, u32[]{:S(2)}) %all-to-all-start) | async-done | bytes 5242912 | tf_op jit(solution)/shard_map/all_to_all | solution.py:22
  308.9 8.8 %fusion.72 = (f32[512]{0:T(512)S(1)}, f32[512,594]{0,1:T(8,128)}) fusion(bf16[512,5120]{1,0:T(8,128)(2,1)} %bitcast.24, bf16[5120,594]{0,1:T(8,128)(2,1)} %param.21), kind=kOutput, calls=%fused_computation.122 | convolution fusion | flops 3114574336 | bytes 12544000 | tf_op jit(solution)/shard_map/dot_general | solution.py:184
  317.7 66.5 %pmax.7 = f32[512]{0:T(512)} all-reduce(f32[512]{0:T(512)S(1)} %get-tuple-element.123), channel_id=1, replica_groups=mesh['req'=32,'tp'=4] {'req','tp'}, use_global_device_ids=true, to_apply=%region_11.12 | all-reduce | flops 512 | bytes 4096 | tf_op jit(solution)/shard_map/pmax | solution.py:185
  (158 shorter events, 85.9 us)
Async XLA Ops:
  7.2 31.7 %copy-start = (bf16[5120,256]{1,0:T(8,128)(2,1)S(1)}, bf16[5120,256]{1,0:T(8,128)(2,1)}, u32[]{:S(2)}) copy-start(bf16[5120,256]{1,0:T(8,128)(2,1)} %param.16) | copy-start | bytes 7864324
  7.2 3.3 copy-start.10
  7.2 3.5 copy-start.8
  7.2 222.1 %all-reduce.3.cloned.1.call-start = ((), (), s32[]{:S(2)}) async-start(), calls=%async_computation.1 | async-start | bytes 7864320 | tf_op jit(solution)/shard_map/psum | solution.py:178
  10.6 5.5 %copy-start.12 = (bf16[5120,640]{1,0:T(8,128)(2,1)S(1)}, bf16[5120,640]{1,0:T(8,128)(2,1)}, u32[]{:S(2)}) copy-start(bf16[5120,640]{1,0:T(8,128)(2,1)} %param.14) | copy-start | bytes 19660804
  10.7 5.5 %copy-start.13 = (f32[640]{0:T(1024)S(1)}, f32[640]{0:T(1024)}, u32[]{:S(2)}) copy-start(f32[640]{0:T(1024)} %param.15) | copy-start | bytes 7684
  14.2 1.9 copy-start.4
  30.0 8.8 %copy-start.14 = (f32[256]{0:T(256)S(1)}, f32[256]{0:T(256)}, u32[]{:S(2)}) copy-start(f32[256]{0:T(256)} %param.17) | copy-start | bytes 3076
  45.7 81.1 %copy-start.5 = (f32[1920,64]{1,0:T(8,128)S(1)}, f32[1920,64]{1,0:T(8,128)}, u32[]{:S(2)}) copy-start(f32[1920,64]{1,0:T(8,128)} %concatenate.59) | copy-start | bytes 1474564
  45.7 81.1 %copy-start.6 = (f32[1920,64]{1,0:T(8,128)S(1)}, f32[1920,64]{1,0:T(8,128)}, u32[]{:S(2)}) copy-start(f32[1920,64]{1,0:T(8,128)} %concatenate.60) | copy-start | bytes 1474564
  58.3 4.2 %copy-start.2 = (bf16[4,3072,1,256]{3,1,2,0:T(8,128)(2,1)S(1)}, bf16[4,3072,1,256]{3,1,2,0:T(8,128)(2,1)}, u32[]{:S(2)}) copy-start(bf16[4,3072,1,256]{3,1,2,0:T(8,128)(2,1)} %get-tuple-element.216) | copy-start | bytes 18874372 | tf_op jit(solution)/shard_map/while
  78.4 4.3 %copy-start.2 = (bf16[4,3072,1,256]{3,1,2,0:T(8,128)(2,1)S(1)}, bf16[4,3072,1,256]{3,1,2,0:T(8,128)(2,1)}, u32[]{:S(2)}) copy-start(bf16[4,3072,1,256]{3,1,2,0:T(8,128)(2,1)} %get-tuple-element.216) | copy-start | bytes 18874372 | tf_op jit(solution)/shard_map/while
  98.5 4.3 %copy-start.2 = (bf16[4,3072,1,256]{3,1,2,0:T(8,128)(2,1)S(1)}, bf16[4,3072,1,256]{3,1,2,0:T(8,128)(2,1)}, u32[]{:S(2)}) copy-start(bf16[4,3072,1,256]{3,1,2,0:T(8,128)(2,1)} %get-tuple-element.216) | copy-start | bytes 18874372 | tf_op jit(solution)/shard_map/while
  118.6 4.3 %copy-start.2 = (bf16[4,3072,1,256]{3,1,2,0:T(8,128)(2,1)S(1)}, bf16[4,3072,1,256]{3,1,2,0:T(8,128)(2,1)}, u32[]{:S(2)}) copy-start(bf16[4,3072,1,256]{3,1,2,0:T(8,128)(2,1)} %get-tuple-element.216) | copy-start | bytes 18874372 | tf_op jit(solution)/shard_map/while
  126.8 1.5 copy-start.7
  137.4 99.1 %copy-start.9 = (f32[5120]{0:T(1024)S(1)}, f32[5120]{0:T(1024)}, u32[]{:S(2)}) copy-start(f32[5120]{0:T(1024)} %param.20) | copy-start | bytes 61444
  234.1 2.0 copy-start.3
  236.5 3.1 copy-start.11
  239.6 69.2 %all-to-all-start = ((bf16[32,16,5120]{2,1,0:T(8,128)(2,1)}), bf16[32,16,5120]{2,1,0:T(8,128)(2,1)}, u32[]{:S(2)}, u32[]{:S(2)}) async-start(bf16[32,16,5120]{2,1,0:T(8,128)(2,1)} %tile.2), calls=%async_computation | async-start | bytes 10485760 | tf_op jit(solution)/shard_map/all_to_all | solution.py:22
  308.9 75.4 %copy-start.1 = (bf16[5120,256]{1,0:T(8,128)(2,1)S(1)}, bf16[5120,256]{1,0:T(8,128)(2,1)}, u32[]{:S(2)}) copy-start(bf16[5120,256]{1,0:T(8,128)(2,1)} %param.16) | copy-start | bytes 7864324
Sparse Core Ops, SparseCore 0:
  137.5 91.7 all-reduce.2
